TPU v7x, 32 devices: a whole 2x2x4 slice. The times are simulated.
32 devices in a mesh: groups: 2 (over x), tm: 4 (over y, core), chan: 4 (over z).
Axes of the slice: x: 2, y: 2, z: 4, core: 2. Of those that a mesh axis runs over, the one named last changes fastest.
Arguments:
- records: bfloat16 [1536, 1024], P(('groups', 'tm'), 'chan'), parts along dimension 0, may hold values from -6 to 6
- cotangent: bfloat16 [1536, 1024], P(('groups', 'tm'), 'chan'), parts along dimension 0, may hold values from -6 to 6
- filter_weight: bfloat16 [4, 2, 1024, 1024], P(None, None, 'tm', 'chan'), may hold values from -0.125 to 0.125
- gate_weight: bfloat16 [4, 2, 1024, 1024], P(None, None, 'tm', 'chan'), may hold values from -0.125 to 0.125
- mix_weight: bfloat16 [4, 1024, 1024], P(None, 'chan', 'tm'), may hold values from -0.1875 to 0.1875
Outputs:
- output: bfloat16 [1536, 1024], P(('groups', 'tm'), 'chan'), parts along dimension 0
- input_grad: bfloat16 [1536, 1024], P(('groups', 'tm'), 'chan'), parts along dimension 0
There are 2 independent parts, one for each index of `groups`. A program takes and returns all parts, laid end to end along the dimension named above; an argument that names none is the same for every part. Nothing has to cross between parts.
All inputs are finite; a program needn't handle non-finite values.
Results may differ from a plain program's by a relative error of at most 0.018.
Values may be sent and summed in bfloat16 or wider, within the bound.
A program may use at most 64 MiB of HBM per device.

v0:
```python
import jax
import jax.numpy as jnp
from jax import lax
from jax.sharding import PartitionSpec as P


def shifted(shard, axis, by):
    peers = lax.axis_size(axis)
    pairs = [(i, i + by) for i in range(peers) if 0 <= i + by < peers]
    return lax.ppermute(shard, axis, pairs)


def right_product(left, panel):
    return lax.dot_general(
        left, panel, (((1,), (1,)), ((), ())), preferred_element_type=jnp.float32
    )


def local(records, cotangent, filter_weight, gate_weight, mix_weight):
    layer_count = filter_weight.shape[0]
    tm_count = lax.axis_size("tm")
    signal = records
    stored = []
    for layer_index in range(layer_count):
        span_shards = 2**layer_index
        filt_panel, gate_panel, mix_panel = (
            lax.all_gather(filter_weight[layer_index], "tm", axis=1, tiled=True),
            lax.all_gather(gate_weight[layer_index], "tm", axis=1, tiled=True),
            lax.all_gather(mix_weight[layer_index], "tm", axis=1, tiled=True),
        )
        whole_rows = lax.all_gather(signal, "chan", axis=1, tiled=True)
        if span_shards < tm_count:
            earlier = shifted(whole_rows, "tm", span_shards)
        else:
            earlier = jnp.zeros_like(whole_rows)
        pre_filter = jnp.dot(earlier, filt_panel[0], preferred_element_type=jnp.float32) + jnp.dot(
            whole_rows, filt_panel[1], preferred_element_type=jnp.float32
        )
        pre_gate = jnp.dot(earlier, gate_panel[0], preferred_element_type=jnp.float32) + jnp.dot(
            whole_rows, gate_panel[1], preferred_element_type=jnp.float32
        )
        gated = (jnp.tanh(pre_filter) * jax.nn.sigmoid(pre_gate)).astype(jnp.bfloat16)
        mix_term = jnp.dot(gated, mix_panel, preferred_element_type=jnp.float32)
        mixed = lax.psum_scatter(
            mix_term.astype(jnp.bfloat16), "chan", scatter_dimension=1, tiled=True
        ).astype(jnp.float32)
        signal = (signal.astype(jnp.float32) + mixed).astype(jnp.bfloat16)
        stored.append((pre_filter, pre_gate, filt_panel, gate_panel, mix_panel))
    grad_now = cotangent
    for layer_index in reversed(range(layer_count)):
        span_shards = 2**layer_index
        pre_filter, pre_gate, filt_panel, gate_panel, mix_panel = stored[layer_index]
        grad_whole = lax.all_gather(grad_now, "chan", axis=1, tiled=True)
        grad_z = right_product(grad_whole, mix_panel)
        tanh_value = jnp.tanh(pre_filter)
        sig_value = jax.nn.sigmoid(pre_gate)
        grad_filt = (grad_z * sig_value * (1.0 - tanh_value * tanh_value)).astype(jnp.bfloat16)
        grad_gate = (grad_z * tanh_value * sig_value * (1.0 - sig_value)).astype(jnp.bfloat16)
        near_term = right_product(grad_filt, filt_panel[1]) + right_product(
            grad_gate, gate_panel[1]
        )
        far_term = right_product(grad_filt, filt_panel[0]) + right_product(grad_gate, gate_panel[0])
        if span_shards < tm_count:
            advanced = shifted(far_term.astype(jnp.bfloat16), "tm", -span_shards).astype(
                far_term.dtype
            )
        else:
            advanced = jnp.zeros_like(far_term)
        returned = lax.psum_scatter(
            (near_term + advanced).astype(jnp.bfloat16), "chan", scatter_dimension=1, tiled=True
        ).astype(jnp.float32)
        grad_now = (grad_now.astype(jnp.float32) + returned).astype(jnp.bfloat16)
    return (signal, grad_now)


def solution(mesh):
    return jax.shard_map(
        local,
        mesh=mesh,
        in_specs=(
            P(("groups", "tm"), "chan"),
            P(("groups", "tm"), "chan"),
            P(None, None, "tm", "chan"),
            P(None, None, "tm", "chan"),
            P(None, "chan", "tm"),
        ),
        out_specs=(P(("groups", "tm"), "chan"), P(("groups", "tm"), "chan")),
        check_vma=False,
    )
```

profile of v0, /device:TPU:0, one launch (start us, length us, event | category | flops | bytes accessed | tf_op | source)
XLA Modules:
  0.0 409.4 jit_solution(5573307418238194053)
XLA Ops:
  7.2 2.3 fusion.67
  10.7 16.4 %all_gather.60 = bf16[192,1024]{1,0:T(8,128)(2,1)S(1)} all-gather(bf16[192,256]{1,0:T(8,128)(2,1)S(1)} %copy-done.34), channel_id=1, replica_groups=mesh['groups'=2,'tm'=4,'chan'=4] {'chan'}, dimensions={1}, use_global_device_ids=true | all-gather | bytes 491520 | tf_op jit(solution)/shard_map/all_gather | solution.py:31
  29.2 7.7 %all-gather.2 = bf16[1,256,1024]{2,1,0:T(8,128)(2,1)S(1)} all-gather(bf16[1,256,256]{2,1,0:T(8,128)(2,1)S(1)} %get-tuple-element.14), channel_id=4, replica_groups=mesh['groups'=2,'tm'=4,'chan'=4] {'tm'}, dimensions={2}, use_global_device_ids=true | all-gather | bytes 655360 | tf_op jit(solution)/shard_map/all_gather | solution.py:29
  38.3 9.2 %all-gather.23.cloned.1.call-done = bf16[1,2,1024,256]{3,2,1,0:T(8,128)(2,1)} async-done(((bf16[1,2,256,256]{3,2,1,0:T(8,128)(2,1)}), bf16[1,2,1024,256]{3,2,1,0:T(8,128)(2,1)}) %all-gather.23.cloned.1.call-update) | async-done | bytes 1048592 | tf_op jit(solution)/shard_map/all_gather | solution.py:28
  54.1 7.2 %all-gather.5 = bf16[1,256,1024]{2,1,0:T(8,128)(2,1)S(1)} all-gather(bf16[1,256,256]{2,1,0:T(8,128)(2,1)S(1)} %get-tuple-element.15), channel_id=7, replica_groups=mesh['groups'=2,'tm'=4,'chan'=4] {'tm'}, dimensions={2}, use_global_device_ids=true | all-gather | bytes 655360 | tf_op jit(solution)/shard_map/all_gather | solution.py:29
  61.3 11.6 %reduce-scatter.9.cloned.1.call-done = bf16[192,256]{1,0:T(8,128)(2,1)} async-done(((bf16[192,1024]{1,0:T(8,128)(2,1)}), bf16[192,256]{1,0:T(8,128)(2,1)}) %reduce-scatter.9.cloned.1.call-update) | async-done | bytes 98320 | tf_op jit(solution)/shard_map/reduce_scatter | solution.py:44
  73.9 14.3 %all_gather.64 = bf16[192,1024]{1,0:T(8,128)(2,1)S(1)} all-gather(bf16[192,256]{1,0:T(8,128)(2,1)S(1)} %add_convert_fusion.9), channel_id=1, replica_groups=mesh['groups'=2,'tm'=4,'chan'=4] {'chan'}, dimensions={1}, use_global_device_ids=true | all-gather | bytes 491520 | tf_op jit(solution)/shard_map/all_gather | solution.py:31
  88.2 4.1 %collective-permute-start.1 = (bf16[192,1024]{1,0:T(8,128)(2,1)S(1)}, bf16[192,1024]{1,0:T(8,128)(2,1)}, u32[]{:S(2)}, u32[]{:S(2)}) collective-permute-start(bf16[192,1024]{1,0:T(8,128)(2,1)S(1)} %all_gather.64), channel_id=1, source_target_pairs={{0,8},{4,12},{1,9},{5,13},{2,10},{6,14},{3,11},{7,15},{16,24},{20,... | collective-permute-start | bytes 1179656 | tf_op jit(solution)/shard_map/ppermute | solution.py:10
  92.3 2.1 fusion.46
  94.4 14.1 %all-gather.27.cloned.1.call-done = bf16[1,2,1024,256]{3,2,1,0:T(8,128)(2,1)} async-done(((bf16[1,2,256,256]{3,2,1,0:T(8,128)(2,1)}), bf16[1,2,1024,256]{3,2,1,0:T(8,128)(2,1)}) %all-gather.27.cloned.1.call-update) | async-done | bytes 1048592 | tf_op jit(solution)/shard_map/all_gather | solution.py:28
  116.1 10.4 %all-gather.11 = bf16[1,256,1024]{2,1,0:T(8,128)(2,1)S(1)} all-gather(bf16[1,256,256]{2,1,0:T(8,128)(2,1)S(1)} %copy-done.33), channel_id=13, replica_groups=mesh['groups'=2,'tm'=4,'chan'=4] {'tm'}, dimensions={2}, use_global_device_ids=true | all-gather | bytes 655360 | tf_op jit(solution)/shard_map/all_gather | solution.py:29
  126.5 7.3 %all-gather.8 = bf16[1,256,1024]{2,1,0:T(8,128)(2,1)S(1)} all-gather(bf16[1,256,256]{2,1,0:T(8,128)(2,1)S(1)} %copy-done.32), channel_id=10, replica_groups=mesh['groups'=2,'tm'=4,'chan'=4] {'tm'}, dimensions={2}, use_global_device_ids=true | all-gather | bytes 655360 | tf_op jit(solution)/shard_map/all_gather | solution.py:29
  133.8 2.0 fusion.27
  135.8 12.0 %all-gather.31.cloned.1.call-done = bf16[1,2,1024,256]{3,2,1,0:T(8,128)(2,1)} async-done(((bf16[1,2,256,256]{3,2,1,0:T(8,128)(2,1)}), bf16[1,2,1024,256]{3,2,1,0:T(8,128)(2,1)}) %all-gather.31.cloned.1.call-update) | async-done | bytes 1048592 | tf_op jit(solution)/shard_map/all_gather | solution.py:28
  147.8 2.0 fusion.26
  149.8 21.1 %reduce-scatter.11.cloned.1.call-done = bf16[192,256]{1,0:T(8,128)(2,1)} async-done(((bf16[192,1024]{1,0:T(8,128)(2,1)}), bf16[192,256]{1,0:T(8,128)(2,1)}) %reduce-scatter.11.cloned.1.call-update) | async-done | bytes 98320 | tf_op jit(solution)/shard_map/reduce_scatter | solution.py:44
  171.9 14.3 %all_gather.69 = bf16[192,1024]{1,0:T(8,128)(2,1)S(1)} all-gather(bf16[192,256]{1,0:T(8,128)(2,1)S(1)} %add_convert_fusion.8), channel_id=1, replica_groups=mesh['groups'=2,'tm'=4,'chan'=4] {'chan'}, dimensions={1}, use_global_device_ids=true | all-gather | bytes 491520 | tf_op jit(solution)/shard_map/all_gather | solution.py:31
  189.9 14.8 %all_gather.76 = bf16[192,1024]{1,0:T(8,128)(2,1)S(1)} all-gather(bf16[192,256]{1,0:T(8,128)(2,1)S(1)} %copy-done.35), channel_id=1, replica_groups=mesh['groups'=2,'tm'=4,'chan'=4] {'chan'}, dimensions={1}, use_global_device_ids=true | all-gather | bytes 491520 | tf_op jit(solution)/shard_map/all_gather | solution.py:53
  205.8 2.0 fusion.25
  207.7 2.0 fusion.24
  209.8 18.9 %reduce-scatter.13.cloned.1.call-done = bf16[192,256]{1,0:T(8,128)(2,1)} async-done(((bf16[192,1024]{1,0:T(8,128)(2,1)}), bf16[192,256]{1,0:T(8,128)(2,1)}) %reduce-scatter.13.cloned.1.call-update) | async-done | bytes 98320 | tf_op jit(solution)/shard_map/reduce_scatter | solution.py:44
  230.3 14.3 %all_gather.73 = bf16[192,1024]{1,0:T(8,128)(2,1)S(1)} all-gather(bf16[192,256]{1,0:T(8,128)(2,1)S(1)} %add_convert_fusion.7), channel_id=1, replica_groups=mesh['groups'=2,'tm'=4,'chan'=4] {'chan'}, dimensions={1}, use_global_device_ids=true | all-gather | bytes 491520 | tf_op jit(solution)/shard_map/all_gather | solution.py:31
  249.2 19.7 %reduce-scatter.17.cloned.1.call-done = bf16[192,256]{1,0:T(8,128)(2,1)} async-done(((bf16[192,1024]{1,0:T(8,128)(2,1)}), bf16[192,256]{1,0:T(8,128)(2,1)}) %reduce-scatter.17.cloned.1.call-update) | async-done | bytes 98320 | tf_op jit(solution)/shard_map/reduce_scatter | solution.py:69
  270.7 14.3 %all_gather.77 = bf16[192,1024]{1,0:T(8,128)(2,1)S(1)} all-gather(bf16[192,256]{1,0:T(8,128)(2,1)S(1)} %add_convert_fusion.5), channel_id=1, replica_groups=mesh['groups'=2,'tm'=4,'chan'=4] {'chan'}, dimensions={1}, use_global_device_ids=true | all-gather | bytes 491520 | tf_op jit(solution)/shard_map/all_gather | solution.py:53
  288.2 19.6 %reduce-scatter.19.cloned.1.call-done = bf16[192,256]{1,0:T(8,128)(2,1)} async-done(((bf16[192,1024]{1,0:T(8,128)(2,1)}), bf16[192,256]{1,0:T(8,128)(2,1)}) %reduce-scatter.19.cloned.1.call-update) | async-done | bytes 98320 | tf_op jit(solution)/shard_map/reduce_scatter | solution.py:69
  308.8 14.4 %all_gather.78 = bf16[192,1024]{1,0:T(8,128)(2,1)S(1)} all-gather(bf16[192,256]{1,0:T(8,128)(2,1)S(1)} %add_convert_fusion.4), channel_id=1, replica_groups=mesh['groups'=2,'tm'=4,'chan'=4] {'chan'}, dimensions={1}, use_global_device_ids=true | all-gather | bytes 491520 | tf_op jit(solution)/shard_map/all_gather | solution.py:53
  326.8 8.0 %collective-permute-done.2 = bf16[192,1024]{1,0:T(8,128)(2,1)S(1)} collective-permute-done((bf16[192,1024]{1,0:T(8,128)(2,1)S(1)}, bf16[192,1024]{1,0:T(8,128)(2,1)S(1)}, u32[]{:S(2)}, u32[]{:S(2)}) %collective-permute-start.2) | collective-permute-done | bytes 393248 | tf_op jit(solution)/shard_map/ppermute | solution.py:10
  337.9 16.8 %reduce-scatter.21.cloned.1.call-done = bf16[192,256]{1,0:T(8,128)(2,1)} async-done(((bf16[192,1024]{1,0:T(8,128)(2,1)}), bf16[192,256]{1,0:T(8,128)(2,1)}) %reduce-scatter.21.cloned.1.call-update) | async-done | bytes 98320 | tf_op jit(solution)/shard_map/reduce_scatter | solution.py:69
  355.7 16.2 %all_gather.79 = bf16[192,1024]{1,0:T(8,128)(2,1)S(1)} all-gather(bf16[192,256]{1,0:T(8,128)(2,1)S(1)} %add_convert_fusion.3), channel_id=1, replica_groups=mesh['groups'=2,'tm'=4,'chan'=4] {'chan'}, dimensions={1}, use_global_device_ids=true | all-gather | bytes 491520 | tf_op jit(solution)/shard_map/all_gather | solution.py:53
  375.4 2.0 collective-permute-done.3
  379.4 1.6 add_convert_fusion.6
  381.0 20.3 %reduce-scatter.23.cloned.1.call-done = bf16[192,256]{1,0:T(8,128)(2,1)} async-done(((bf16[192,1024]{1,0:T(8,128)(2,1)}), bf16[192,256]{1,0:T(8,128)(2,1)}) %reduce-scatter.23.cloned.1.call-update) | async-done | bytes 98320 | tf_op jit(solution)/shard_map/reduce_scatter | solution.py:69
  (165 shorter events, 52.0 us)
Async XLA Ops:
  7.2 29.7 %all-gather.21.cloned.1.call-start = ((), (), s32[]{:S(2)}) async-start(), calls=%async_computation.16 | async-start | bytes 1310720 | tf_op jit(solution)/shard_map/all_gather | solution.py:27
  9.6 37.9 %all-gather.23.cloned.1.call-start = ((), (), s32[]{:S(2)}) async-start(), calls=%async_computation.17 | async-start | bytes 1310720 | tf_op jit(solution)/shard_map/all_gather | solution.py:28
  10.6 17.8 %copy-start.31 = (bf16[4,256,256]{2,1,0:T(8,128)(2,1)S(1)}, bf16[4,256,256]{2,1,0:T(8,128)(2,1)}, u32[]{:S(2)}) copy-start(bf16[4,256,256]{2,1,0:T(8,128)(2,1)} %param.9) | copy-start | bytes 1572868
  10.7 62.3 %reduce-scatter.9.cloned.1.call-start = ((), (), s32[]{:S(2)}) async-start(), calls=%async_computation.8 | async-start | bytes 491520 | tf_op jit(solution)/shard_map/reduce_scatter | solution.py:44
  27.1 21.7 %collective-permute-start = (bf16[192,1024]{1,0:T(8,128)(2,1)S(1)}, bf16[192,1024]{1,0:T(8,128)(2,1)S(1)}, u32[]{:S(2)}, u32[]{:S(2)}) collective-permute-start(bf16[192,1024]{1,0:T(8,128)(2,1)S(1)} %all_gather.60), channel_id=1, source_target_pairs={{0,4},{4,8},{8,12},{1,5},{5,9},{9,13},{2,6},{6,10},{10,14},{3,7},{... | collective-permute-start | bytes 1179656 | tf_op jit(solution)/shard_map/ppermute | solution.py:10
  51.6 40.7 %all-gather.25.cloned.1.call-start = ((), (), s32[]{:S(2)}) async-start(), calls=%async_computation.18 | async-start | bytes 1310720 | tf_op jit(solution)/shard_map/all_gather | solution.py:27
  52.2 56.3 %all-gather.27.cloned.1.call-start = ((), (), s32[]{:S(2)}) async-start(), calls=%async_computation.19 | async-start | bytes 1310720 | tf_op jit(solution)/shard_map/all_gather | solution.py:28
  52.8 81.0 %all-gather.29.cloned.1.call-start = ((), (), s32[]{:S(2)}) async-start(), calls=%async_computation.20 | async-start | bytes 1310720 | tf_op jit(solution)/shard_map/all_gather | solution.py:27
  53.3 94.4 %all-gather.31.cloned.1.call-start = ((), (), s32[]{:S(2)}) async-start(), calls=%async_computation.21 | async-start | bytes 1310720 | tf_op jit(solution)/shard_map/all_gather | solution.py:28
  54.1 116.8 %reduce-scatter.11.cloned.1.call-start = ((), (), s32[]{:S(2)}) async-start(), calls=%async_computation.9 | async-start | bytes 491520 | tf_op jit(solution)/shard_map/reduce_scatter | solution.py:44
  88.2 21.7 %collective-permute-start.1 = (bf16[192,1024]{1,0:T(8,128)(2,1)S(1)}, bf16[192,1024]{1,0:T(8,128)(2,1)}, u32[]{:S(2)}, u32[]{:S(2)}) collective-permute-start(bf16[192,1024]{1,0:T(8,128)(2,1)S(1)} %all_gather.64), channel_id=1, source_target_pairs={{0,8},{4,12},{1,9},{5,13},{2,10},{6,14},{3,11},{7,15},{16,24},{20,... | collective-permute-start | bytes 1179656 | tf_op jit(solution)/shard_map/ppermute | solution.py:10
  92.3 17.6 %copy-start.1 = (bf16[1,2,1024,256]{3,2,1,0:T(8,128)(2,1)S(1)}, bf16[1,2,1024,256]{3,2,1,0:T(8,128)(2,1)}, u32[]{:S(2)}) copy-start(bf16[1,2,1024,256]{3,2,1,0:T(8,128)(2,1)} %all-gather.25.cloned.1.call-done) | copy-start | bytes 3145732
  114.4 91.3 %all-gather.33.cloned.1.call-start = ((), (), s32[]{:S(2)}) async-start(), calls=%async_computation.22 | async-start | bytes 1310720 | tf_op jit(solution)/shard_map/all_gather | solution.py:27
  115.2 92.6 %all-gather.35.cloned.1.call-start = ((), (), s32[]{:S(2)}) async-start(), calls=%async_computation.23 | async-start | bytes 1310720 | tf_op jit(solution)/shard_map/all_gather | solution.py:28
  115.8 112.9 %reduce-scatter.13.cloned.1.call-start = ((), (), s32[]{:S(2)}) async-start(), calls=%async_computation.10 | async-start | bytes 491520 | tf_op jit(solution)/shard_map/reduce_scatter | solution.py:44
  135.8 35.1 %copy-start.22 = (bf16[192,256]{1,0:T(8,128)(2,1)S(1)}, bf16[192,256]{1,0:T(8,128)(2,1)}, u32[]{:S(2)}) copy-start(bf16[192,256]{1,0:T(8,128)(2,1)} %copy-done.21) | copy-start | bytes 294916
  170.9 16.7 %copy-start.36 = (bf16[1,2,1024,256]{3,2,1,0:T(8,128)(2,1)S(1)}, bf16[1,2,1024,256]{3,2,1,0:T(8,128)(2,1)}, u32[]{:S(2)}) copy-start(bf16[1,2,1024,256]{3,2,1,0:T(8,128)(2,1)} %all-gather.31.cloned.1.call-done) | copy-start | bytes 3145732
  189.0 79.9 %reduce-scatter.17.cloned.1.call-start = ((), (), s32[]{:S(2)}) async-start(), calls=%async_computation.12 | async-start | bytes 491520 | tf_op jit(solution)/shard_map/reduce_scatter | solution.py:69
  207.7 20.9 %copy-start.24 = (bf16[192,256]{1,0:T(8,128)(2,1)S(1)}, bf16[192,256]{1,0:T(8,128)(2,1)}, u32[]{:S(2)}) copy-start(bf16[192,256]{1,0:T(8,128)(2,1)} %copy-done.23) | copy-start | bytes 294916
  228.7 17.3 %copy-start.38 = (bf16[1,2,1024,256]{3,2,1,0:T(8,128)(2,1)S(1)}, bf16[1,2,1024,256]{3,2,1,0:T(8,128)(2,1)}, u32[]{:S(2)}) copy-start(bf16[1,2,1024,256]{3,2,1,0:T(8,128)(2,1)} %all-gather.35.cloned.1.call-done) | copy-start | bytes 3145732
  249.2 58.7 %reduce-scatter.19.cloned.1.call-start = ((), (), s32[]{:S(2)}) async-start(), calls=%async_computation.13 | async-start | bytes 491520 | tf_op jit(solution)/shard_map/reduce_scatter | solution.py:69
  268.9 16.3 %copy-start.17 = (bf16[1,2,1024,256]{3,2,1,0:T(8,128)(2,1)S(1)}, bf16[1,2,1024,256]{3,2,1,0:T(8,128)(2,1)}, u32[]{:S(2)}) copy-start(bf16[1,2,1024,256]{3,2,1,0:T(8,128)(2,1)} %all-gather.29.cloned.1.call-done) | copy-start | bytes 3145732
  288.1 19.7 %copy-start.26 = (bf16[192,256]{1,0:T(8,128)(2,1)S(1)}, bf16[192,256]{1,0:T(8,128)(2,1)}, u32[]{:S(2)}) copy-start(bf16[192,256]{1,0:T(8,128)(2,1)} %copy-done.25) | copy-start | bytes 294916
  288.2 66.6 %reduce-scatter.21.cloned.1.call-start = ((), (), s32[]{:S(2)}) async-start(), calls=%async_computation.14 | async-start | bytes 491520 | tf_op jit(solution)/shard_map/reduce_scatter | solution.py:69
  307.9 15.4 %copy-start.14 = (f32[192,256]{1,0:T(8,128)S(1)}, f32[192,256]{1,0:T(8,128)}, u32[]{:S(2)}) copy-start(f32[192,256]{1,0:T(8,128)} %copy-done.13) | copy-start | bytes 589828
  307.9 15.4 %copy-start.30 = (f32[192,256]{1,0:T(8,128)S(1)}, f32[192,256]{1,0:T(8,128)}, u32[]{:S(2)}) copy-start(f32[192,256]{1,0:T(8,128)} %copy-done.29) | copy-start | bytes 589828
  325.1 9.7 %collective-permute-start.2 = (bf16[192,1024]{1,0:T(8,128)(2,1)S(1)}, bf16[192,1024]{1,0:T(8,128)(2,1)S(1)}, u32[]{:S(2)}, u32[]{:S(2)}) collective-permute-start(bf16[192,1024]{1,0:T(8,128)(2,1)S(1)} %fusion.2), channel_id=1, source_target_pairs={{8,0},{12,4},{9,1},{13,5},{10,2},{14,6},{11,3},{15,7},{24,16},{28,... | collective-permute-start | bytes 1179656 | tf_op jit(solution)/shard_map/ppermute | solution.py:10
  335.9 42.7 %reduce-scatter.15.cloned.1.call-start = ((), (), s32[]{:S(2)}) async-start(), calls=%async_computation.11 | async-start | bytes 491520 | tf_op jit(solution)/shard_map/reduce_scatter | solution.py:44
  337.9 63.5 %reduce-scatter.23.cloned.1.call-start = ((), (), s32[]{:S(2)}) async-start(), calls=%async_computation.15 | async-start | bytes 491520 | tf_op jit(solution)/shard_map/reduce_scatter | solution.py:69
  355.7 16.2 %copy-start.12 = (f32[192,256]{1,0:T(8,128)S(1)}, f32[192,256]{1,0:T(8,128)}, u32[]{:S(2)}) copy-start(f32[192,256]{1,0:T(8,128)} %copy-done.11) | copy-start | bytes 589828
  355.7 16.2 %copy-start.28 = (f32[192,256]{1,0:T(8,128)S(1)}, f32[192,256]{1,0:T(8,128)}, u32[]{:S(2)}) copy-start(f32[192,256]{1,0:T(8,128)} %copy-done.27) | copy-start | bytes 589828
  373.8 3.6 collective-permute-start.3
  (29 other events, 93.6 us)
Sparse Core Ops, SparseCore 0:
  9.7 19.4 all-gather.20
  30.7 16.6 all-gather.22
  51.7 21.1 reduce-scatter.8
  74.3 14.9 all-gather.24
  90.8 17.6 all-gather.26
  109.9 19.4 all-gather.28
  131.0 16.6 all-gather.30
  150.0 20.7 reduce-scatter.10
  172.4 14.9 all-gather.32
  188.8 16.6 all-gather.34
  207.8 20.7 reduce-scatter.12
  249.3 19.6 reduce-scatter.16
  288.3 19.5 reduce-scatter.18
  336.0 18.6 reduce-scatter.20
  356.9 19.8 reduce-scatter.14
  378.9 22.3 reduce-scatter.22
where the time goes:
time: 411 us; the launch traced here: 409 us
  waiting for transfers between devices  177 us (43%)
  blocking collectives  151 us (37%)
  matrix products  34.2 us (8%)
  local copies, waits for them, and re-layouts  14.6 us (4%)
  between operations  14.4 us (4%)
  other arithmetic  8.99 us (2%)
  starting transfers between devices  8.64 us (2%)
    reduce_scatter x4, waiting for transfers between devices, local(): lax.psum_scatter((near_term + advanced).astype(jnp.bfloat16), 'chan', sca...  76.5 us
    all_gather x4, blocking collectives, local(): grad_whole = lax.all_gather(grad_now, 'chan', axis=1, tiled=True)  59.7 us
    all_gather x4, blocking collectives, local(): whole_rows = lax.all_gather(signal, 'chan', axis=1, tiled=True)  59.3 us
    reduce_scatter x4, waiting for transfers between devices, local(): lax.psum_scatter(mix_term.astype(jnp.bfloat16), 'chan', scatter_dimension...  51.7 us
    all_gather x4, waiting for transfers between devices, local(): lax.all_gather(gate_weight[layer_index], 'tm', axis=1, tiled=True)  35.2 us
    all_gather x4, blocking collectives, local(): lax.all_gather(mix_weight[layer_index], 'tm', axis=1, tiled=True)  32.4 us
    unnamed x82, local copies, waits for them, and re-layouts  10.6 us
    ppermute x4, waiting for transfers between devices, shifted(): return lax.ppermute(shard, axis, pairs)  10 us
  transfers between devices with their start and end apart: 20, of which 12 were waited for; matrix products, arithmetic and copies ran while one was open for 8% of the time, Pallas kernels for 0%

commit v1 on v0

v1 whole, which is shorter than its diff:
```python
import functools

import jax
import jax.numpy as jnp
from jax import lax
from jax.experimental import pallas as pl
from jax.experimental.pallas import tpu as pltpu
from jax.sharding import PartitionSpec as P

MESH = pl.DeviceIdType.MESH
DMA = pltpu.SemaphoreType.DMA
BF = jnp.bfloat16
F32 = jnp.float32


def dot(a, b):
    return jnp.dot(a, b, preferred_element_type=F32)


def dot_t(a, b):
    return lax.dot_general(a, b, (((1,), (1,)), ((), ())), preferred_element_type=F32)


def near_first(count):
    order = []
    for step in range(1, count // 2 + 1):
        for offset in (step, count - step):
            if offset not in order and offset < count:
                order.append(offset)
    return order


def kernel(
    layers, tm, chan,
    rec, cot, f_in, g_in, m_in,
    out, gin,
    fw, gw, mw, sig, dly, rsb, rsr, gr, farb, farr, tval, sval, acc_f, acc_g,
    w_send, w_recv, w_fwd, w_own,
    ag_send, ag_recv, d_send, d_recv, rs_send, rs_recv, f_send, f_recv,
):
    m = lax.axis_index("tm")
    c = lax.axis_index("chan")
    ratio = tm // chan
    rows, cb = rec.shape
    ob = mw.shape[-1]
    partner = m + 1 - 2 * lax.rem(m, 2)
    peers = near_first(chan)
    others = list(range(1, tm // 2))

    def peer(r):
        return lax.rem(c + r, chan)

    def mate(q, base=None):
        return lax.rem((m if base is None else base) + 2 * q, tm)

    def span(l):
        return 2**l

    def far(l):
        return span(l) < tm

    def own_block(l, p):
        if p == 2:
            return m_in.at[l]
        w = (f_in, g_in)[p]
        return w.at[l] if far(l) else w.at[l, 1]

    def slot(l, p, s):
        if p == 2:
            return mw.at[l, s]
        w = (fw, gw)[p]
        return w.at[l, :, s] if far(l) else w.at[l, 1, s]

    def w_copy(l, p, s, to, send, own):
        return pltpu.make_async_remote_copy(
            src_ref=own_block(l, p) if own else slot(l, p, s),
            dst_ref=slot(l, p, s),
            send_sem=send,
            recv_sem=w_recv.at[l * 3 + p, s],
            device_id={"tm": to},
            device_id_type=MESH,
        )

    def w_out(l, p, q):
        if q == 0:
            return w_copy(l, p, m, partner, w_send.at[l * 3 + p, 0], True)
        return w_copy(l, p, m, mate(q), w_send.at[l * 3 + p, q], True)

    def w_on(l, p, q):
        return w_copy(l, p, mate(q), partner, w_fwd.at[l * 3 + p, q], False)

    def w_mine(l, p):
        return pltpu.make_async_copy(own_block(l, p), slot(l, p, m), w_own.at[l * 3 + p])

    def w_start(l):
        for p in range(3):
            for q in others + [0]:
                w_out(l, p, q).start()
            w_mine(l, p).start()

    def w_forward(l):
        for p in range(3):
            for q in others:
                w_on(l, p, q).wait_recv()
                w_on(l, p, q).start()

    def w_ready(l, kinds):
        for p in kinds:
            w_mine(l, p).wait()
            w_copy(l, p, partner, partner, w_fwd.at[l * 3 + p, 0], False).wait_recv()
            for q in others:
                s = mate(q, partner)
                w_copy(l, p, s, partner, w_fwd.at[l * 3 + p, 0], False).wait_recv()

    def ag(i, src, buf, l, r, owner):
        return pltpu.make_async_remote_copy(
            src_ref=src,
            dst_ref=buf.at[l, owner],
            send_sem=ag_send.at[i, r],
            recv_sem=ag_recv.at[i, owner],
            device_id={"chan": peer(r)},
            device_id_type=MESH,
        )

    def ag_start(i, src, buf, l):
        for r in reversed(peers):
            ag(i, src, buf, l, r, c).start()

    def ag_wait(i, buf, l, r):
        ag(i, buf.at[l, c], buf, l, r, peer(r)).wait_recv()

    def rs(i, r, owner):
        return pltpu.make_async_remote_copy(
            src_ref=rsb.at[i, r],
            dst_ref=rsr.at[i, owner],
            send_sem=rs_send.at[i, r],
            recv_sem=rs_recv.at[i, owner],
            device_id={"chan": peer(r)},
            device_id_type=MESH,
        )

    def dl(l, j):
        return pltpu.make_async_remote_copy(
            src_ref=sig.at[l, j],
            dst_ref=dly.at[l, j],
            send_sem=d_send.at[l, j],
            recv_sem=d_recv.at[l, j],
            device_id={"tm": lax.rem(m + span(l), tm)},
            device_id_type=MESH,
        )

    def fr(l, j):
        return pltpu.make_async_remote_copy(
            src_ref=farb.at[l, j],
            dst_ref=farr.at[l, j],
            send_sem=f_send.at[l, j],
            recv_sem=f_recv.at[l, j],
            device_id={"tm": lax.rem(m + tm - span(l), tm)},
            device_id_type=MESH,
        )

    def block(w, l, tap, j):
        return w[l, tap, pl.ds(j * ratio, ratio)].reshape(cb, cb)

    barrier = pltpu.get_barrier_semaphore()
    for s in range(1, tm):
        pl.semaphore_signal(barrier, inc=1, device_id={"tm": lax.rem(m + s, tm)}, device_id_type=MESH)
    for s in range(1, chan):
        pl.semaphore_signal(barrier, inc=1, device_id={"chan": peer(s)}, device_id_type=MESH)
    pl.semaphore_wait(barrier, tm - 1 + chan - 1)

    ag_start(0, rec, sig, 0)
    w_start(0)
    sig[0, c] = rec[...]
    gr[layers - 1, c] = cot[...]
    for l in range(1, layers):
        w_start(l)
    ag_start(layers, cot, gr, layers - 1)

    for l in range(layers):
        if l > 0:
            ag_start(l, sig.at[l, c], sig, l)
        if far(l):
            @pl.when(m < tm - span(l))
            def _():
                dl(l, c).start()
                for r in peers:
                    ag_wait(l, sig, l, r)
                    dl(l, peer(r)).start()

            @pl.when(m >= tm - span(l))
            def _():
                for r in peers:
                    ag_wait(l, sig, l, r)
        if l == 0:
            w_forward(0)
            w_ready(0, (0, 1))
        else:
            w_ready(l, (0, 1))
        for r in [0] + peers:
            j = peer(r)
            if r and not far(l):
                ag_wait(l, sig, l, r)
            x = sig[l, j]
            a = dot(x, block(fw, l, 1, j))
            b = dot(x, block(gw, l, 1, j))
            if r == 0:
                acc_f[...] = a
                acc_g[...] = b
            else:
                acc_f[...] += a
                acc_g[...] += b
        if far(l):
            @pl.when(m >= span(l))
            def _():
                for r in [0] + peers:
                    j = peer(r)
                    dl(l, j).wait_recv()
                    x = dly[l, j]
                    acc_f[...] += dot(x, block(fw, l, 0, j))
                    acc_g[...] += dot(x, block(gw, l, 0, j))
        th = jnp.tanh(acc_f[...])
        sg = jax.nn.sigmoid(acc_g[...])
        tval[l] = th
        sval[l] = sg
        gated = (th * sg).astype(BF)
        w_ready(l, (2,))

        def mixed(j):
            parts = [dot(gated, mw[l, j * ratio + i]) for i in range(ratio)]
            return parts[0] if ratio == 1 else jnp.concatenate(parts, axis=1)

        for r in reversed(peers):
            rsb[l, r] = mixed(peer(r)).astype(BF)
            rs(l, r, c).start()
        acc_f[...] = mixed(c) + sig[l, c].astype(F32)
        if l + 1 < layers:
            w_forward(l + 1)
        for r in peers:
            rs(l, r, peer(r)).wait_recv()
            acc_f[...] += rsr[l, peer(r)].astype(F32)
        if l + 1 < layers:
            sig[l + 1, c] = acc_f[...].astype(BF)
        else:
            out[...] = acc_f[...].astype(BF)

    for l in reversed(range(layers)):
        i = 2 * layers - 1 - l
        if l < layers - 1:
            ag_start(i, gr.at[l, c], gr, l)
        for r in [0] + peers:
            j = peer(r)
            if r:
                ag_wait(i, gr, l, r)
            g = gr[l, j]
            for k in range(ratio):
                z = dot_t(g[:, k * ob:(k + 1) * ob], mw[l, j * ratio + k])
                if r == 0 and k == 0:
                    acc_f[...] = z
                else:
                    acc_f[...] += z
        gz = acc_f[...]
        th = tval[l]
        sg = sval[l]
        gf = (gz * sg * (1.0 - th * th)).astype(BF)
        gg = (gz * th * sg * (1.0 - sg)).astype(BF)
        order = list(reversed(peers)) + [0]
        if far(l):
            @pl.when(m >= span(l))
            def _():
                for r in order:
                    j = peer(r)
                    farb[l, j] = (dot_t(gf, block(fw, l, 0, j)) + dot_t(gg, block(gw, l, 0, j))).astype(BF)
                    fr(l, j).start()
        for r in order:
            j = peer(r)
            acc_g[...] = dot_t(gf, block(fw, l, 1, j)) + dot_t(gg, block(gw, l, 1, j))
            if far(l):
                @pl.when(m < tm - span(l))
                def _():
                    fr(l, j).wait_recv()
                    acc_g[...] += farr[l, j].astype(F32)
            if r:
                rsb[i, r] = acc_g[...].astype(BF)
                rs(i, r, c).start()
        acc_f[...] = acc_g[...] + gr[l, c].astype(F32)
        for r in peers:
            rs(i, r, peer(r)).wait_recv()
            acc_f[...] += rsr[i, peer(r)].astype(F32)
        if l > 0:
            gr[l - 1, c] = acc_f[...].astype(BF)
        else:
            gin[...] = acc_f[...].astype(BF)

    for l in range(layers):
        for p in range(3):
            for q in others:
                w_out(l, p, q).wait_send()
                w_on(l, p, q).wait_send()
            w_out(l, p, 0).wait_send()
        if far(l):
            @pl.when(m < tm - span(l))
            def _():
                for j in range(chan):
                    dl(l, j).wait_send()

            @pl.when(m >= span(l))
            def _():
                for j in range(chan):
                    fr(l, j).wait_send()
    for i in range(2 * layers):
        for r in peers:
            ag(i, rec, sig, 0, r, c).wait_send()
            rs(i, r, c).wait_send()


def local(records, cotangent, filter_weight, gate_weight, mix_weight):
    tm, chan = lax.axis_size("tm"), lax.axis_size("chan")
    layers, taps, ib, cb = filter_weight.shape
    ob = mix_weight.shape[2]
    rows = records.shape[0]
    vmem = pl.BlockSpec(memory_space=pltpu.VMEM)
    hbm = pl.BlockSpec(memory_space=pl.ANY)
    weights = pltpu.VMEM((layers, taps, tm, ib, cb), BF)
    per_layer = pltpu.VMEM((layers, chan, rows, cb), BF)
    both = pltpu.VMEM((2 * layers, chan, rows, cb), BF)
    return pl.pallas_call(
        functools.partial(kernel, layers, tm, chan),
        out_shape=[jax.ShapeDtypeStruct(records.shape, BF)] * 2,
        in_specs=[vmem, vmem, hbm, hbm, hbm],
        out_specs=[vmem, vmem],
        scratch_shapes=[
            weights,
            weights,
            pltpu.VMEM((layers, tm, cb, ob), BF),
            per_layer,
            per_layer,
            both,
            both,
            per_layer,
            per_layer,
            per_layer,
            pltpu.VMEM((layers, rows, cb), F32),
            pltpu.VMEM((layers, rows, cb), F32),
            pltpu.VMEM((rows, cb), F32),
            pltpu.VMEM((rows, cb), F32),
            DMA((3 * layers, tm)),
            DMA((3 * layers, tm)),
            DMA((3 * layers, tm)),
            DMA((3 * layers,)),
            DMA((2 * layers, chan)),
            DMA((2 * layers, chan)),
            DMA((layers, chan)),
            DMA((layers, chan)),
            DMA((2 * layers, chan)),
            DMA((2 * layers, chan)),
            DMA((layers, chan)),
            DMA((layers, chan)),
        ],
        compiler_params=pltpu.CompilerParams(
            collective_id=0, has_side_effects=True, vmem_limit_bytes=56 * 2**20
        ),
    )(records, cotangent, filter_weight, gate_weight, mix_weight)


def solution(mesh):
    return jax.shard_map(
        local,
        mesh=mesh,
        in_specs=(
            P(("groups", "tm"), "chan"),
            P(("groups", "tm"), "chan"),
            P(None, None, "tm", "chan"),
            P(None, None, "tm", "chan"),
            P(None, "chan", "tm"),
        ),
        out_specs=(P(("groups", "tm"), "chan"), P(("groups", "tm"), "chan")),
        check_vma=False,
    )
```

time: 411 us -> 199 us (0.48)
  Pallas kernels: 0 us -> 192 us
  waiting for transfers between devices: 177 us -> 0 us
  blocking collectives: 151 us -> 0 us
  matrix products: 34.2 us -> 0 us
  between operations: 14.4 us -> 0.65 us
  local copies, waits for them, and re-layouts: 14.6 us -> 2.22 us
  other arithmetic: 8.99 us -> 0 us
  starting transfers between devices: 8.64 us -> 0 us
    pallas_call x0 -> x1, Pallas kernels: none -> 192 us  [local(): pl.pallas_call(functools.partial(kernel, layers, tm, chan), out_shape=[ja...]
    all_gather x12 -> x0, blocking collectives: 151 us -> none  [the longest x4 59.7 us: local(): grad_whole = lax.all_gather(grad_now, 'chan', axis=1, tiled=True)]
    reduce_scatter x8 -> x0, waiting for transfers between devices: 128 us -> none  [the longest x4 76.5 us: local(): lax.psum_scatter((near_term + advanced).astype(jnp.bfloat16), 'chan', sca...]
    all_gather x8 -> x0, waiting for transfers between devices: 35.3 us -> none  [the longest x4 35.2 us: local(): lax.all_gather(gate_weight[layer_index], 'tm', axis=1, tiled=True)]
    dot_general x36 -> x0, matrix products: 34.2 us -> none  [the longest x16 9.03 us: right_product(): lax.dot_general(left, panel, (((1,), (1,)), ((), ())), preferred_element_...]
    ppermute x4 -> x0, waiting for transfers between devices: 10 us -> none  [shifted(): return lax.ppermute(shard, axis, pairs)]
    convert_element_type x8 -> x0, other arithmetic: 8.99 us -> none  [the longest x4 4.5 us: local(): grad_now = (grad_now.astype(jnp.float32) + returned).astype(jnp.bfloat16)]
    unnamed x82 -> x4, local copies, waits for them, and re-layouts: 10.6 us -> 2.22 us
  transfers between devices with their start and end apart: 20 -> 0, of which waited for: 12 -> 0; matrix products, arithmetic and copies ran while one was open for 8% -> 0% of each run, Pallas kernels for 0% -> 0%
where the time goes in v1:
time: 199 us; the launch traced here: 195 us
  Pallas kernels  192 us (96%)
  local copies, waits for them, and re-layouts  2.22 us (1%)
    pallas_call x1, Pallas kernels, local(): pl.pallas_call(functools.partial(kernel, layers, tm, chan), out_shape=[ja...  192 us

profile of v1, /device:TPU:0, one launch (start us, length us, event | category | flops | bytes accessed | tf_op | source)
XLA Modules:
  0.0 195.0 jit_solution(7398058256362421628)
XLA Ops:
  0.6 192.2 %shard_map.68 = (bf16[192,256]{1,0:T(8,128)(2,1)}, bf16[192,256]{1,0:T(8,128)(2,1)}) custom-call(bf16[192,256]{1,0:T(8,128)(2,1)} %rec.1, bf16[192,256]{1,0:T(8,128)(2,1)} %cot.1, bf16[4,2,256,256]{3,2,1,0:T(8,128)(2,1)} %f_in.1, bf16[4,2,256,256]{3,2,1,0:T(8,128)(2,1)} %g_in.1, bf16[4,256,256]{2,1,0:T(8,128)(2,1)} %m_in.1), custom_call_target="tpu_custom_call" | custom-call | tf_op jit(solution)/shard_map/pallas_call | solution.py:327
  192.8 0.0 copy-start
  192.8 1.6 copy.9
  194.4 0.0 copy-done
  194.4 0.6 copy.10
Async XLA Ops:
  192.8 1.6 copy-start

commit v2 on v1

--- a/solution.py
+++ b/solution.py
@@ -11,6 +11,7 @@
 DMA = pltpu.SemaphoreType.DMA
 BF = jnp.bfloat16
 F32 = jnp.float32
+H = 2
 
 
 def dot(a, b):
@@ -34,7 +35,7 @@
     layers, tm, chan,
     rec, cot, f_in, g_in, m_in,
     out, gin,
-    fw, gw, mw, sig, dly, rsb, rsr, gr, farb, farr, tval, sval, acc_f, acc_g,
+    fw, gw, mw, sig, dly, rsb, rsr, gr, farb, farr, tval, sval, acc_f, acc_g, gf_s, gg_s,
     w_send, w_recv, w_fwd, w_own,
     ag_send, ag_recv, d_send, d_recv, rs_send, rs_recv, f_send, f_recv,
 ):
@@ -43,6 +44,7 @@
     ratio = tm // chan
     rows, cb = rec.shape
     ob = mw.shape[-1]
+    half = rows // H
     partner = m + 1 - 2 * lax.rem(m, 2)
     peers = near_first(chan)
     others = list(range(1, tm // 2))
@@ -98,8 +100,8 @@
                 w_out(l, p, q).start()
             w_mine(l, p).start()
 
-    def w_forward(l):
-        for p in range(3):
+    def w_forward(l, kinds):
+        for p in kinds:
             for q in others:
                 w_on(l, p, q).wait_recv()
                 w_on(l, p, q).start()
@@ -139,22 +141,24 @@
             device_id_type=MESH,
         )
 
-    def dl(l, j):
+    def dl(l, hh, j):
+        n = l * H + hh
         return pltpu.make_async_remote_copy(
-            src_ref=sig.at[l, j],
-            dst_ref=dly.at[l, j],
-            send_sem=d_send.at[l, j],
-            recv_sem=d_recv.at[l, j],
+            src_ref=sig.at[n, j],
+            dst_ref=dly.at[n, j],
+            send_sem=d_send.at[n, j],
+            recv_sem=d_recv.at[n, j],
             device_id={"tm": lax.rem(m + span(l), tm)},
             device_id_type=MESH,
         )
 
-    def fr(l, j):
+    def fr(l, hh, j):
+        n = l * H + hh
         return pltpu.make_async_remote_copy(
-            src_ref=farb.at[l, j],
-            dst_ref=farr.at[l, j],
-            send_sem=f_send.at[l, j],
-            recv_sem=f_recv.at[l, j],
+            src_ref=farb.at[n, j],
+            dst_ref=farr.at[n, j],
+            send_sem=f_send.at[n, j],
+            recv_sem=f_recv.at[n, j],
             device_id={"tm": lax.rem(m + tm - span(l), tm)},
             device_id_type=MESH,
         )
@@ -169,128 +173,178 @@
         pl.semaphore_signal(barrier, inc=1, device_id={"chan": peer(s)}, device_id_type=MESH)
     pl.semaphore_wait(barrier, tm - 1 + chan - 1)
 
-    ag_start(0, rec, sig, 0)
+    def part(hh):
+        return pl.ds(hh * half, half)
+
+    for hh in range(H):
+        ag_start(hh, rec.at[part(hh)], sig, hh)
     w_start(0)
-    sig[0, c] = rec[...]
-    gr[layers - 1, c] = cot[...]
+    for hh in range(H):
+        sig[hh, c] = rec[hh * half:(hh + 1) * half]
+        gr[(layers - 1) * H + hh, c] = cot[hh * half:(hh + 1) * half]
     for l in range(1, layers):
         w_start(l)
-    ag_start(layers, cot, gr, layers - 1)
-
-    for l in range(layers):
-        if l > 0:
-            ag_start(l, sig.at[l, c], sig, l)
+    for hh in range(H):
+        ag_start(layers * H + hh, cot.at[part(hh)], gr, (layers - 1) * H + hh)
+
+    def near_taps(l, hh):
+        n = l * H + hh
         if far(l):
             @pl.when(m < tm - span(l))
             def _():
-                dl(l, c).start()
+                dl(l, hh, c).start()
                 for r in peers:
-                    ag_wait(l, sig, l, r)
-                    dl(l, peer(r)).start()
+                    ag_wait(n, sig, n, r)
+                    dl(l, hh, peer(r)).start()
 
             @pl.when(m >= tm - span(l))
             def _():
                 for r in peers:
-                    ag_wait(l, sig, l, r)
-        if l == 0:
-            w_forward(0)
-            w_ready(0, (0, 1))
-        else:
+                    ag_wait(n, sig, n, r)
+        if hh == 0:
+            if l == 0:
+                w_forward(0, (0, 1))
             w_ready(l, (0, 1))
         for r in [0] + peers:
             j = peer(r)
             if r and not far(l):
-                ag_wait(l, sig, l, r)
-            x = sig[l, j]
+                ag_wait(n, sig, n, r)
+            x = sig[n, j]
             a = dot(x, block(fw, l, 1, j))
             b = dot(x, block(gw, l, 1, j))
             if r == 0:
-                acc_f[...] = a
-                acc_g[...] = b
+                acc_f[hh] = a
+                acc_g[hh] = b
             else:
-                acc_f[...] += a
-                acc_g[...] += b
+                acc_f[hh] += a
+                acc_g[hh] += b
+
+    def mix_out(l, hh):
+        n = l * H + hh
         if far(l):
             @pl.when(m >= span(l))
             def _():
                 for r in [0] + peers:
                     j = peer(r)
-                    dl(l, j).wait_recv()
-                    x = dly[l, j]
-                    acc_f[...] += dot(x, block(fw, l, 0, j))
-                    acc_g[...] += dot(x, block(gw, l, 0, j))
-        th = jnp.tanh(acc_f[...])
-        sg = jax.nn.sigmoid(acc_g[...])
-        tval[l] = th
-        sval[l] = sg
+                    dl(l, hh, j).wait_recv()
+                    x = dly[n, j]
+                    acc_f[hh] += dot(x, block(fw, l, 0, j))
+                    acc_g[hh] += dot(x, block(gw, l, 0, j))
+        th = jnp.tanh(acc_f[hh])
+        sg = jax.nn.sigmoid(acc_g[hh])
+        tval[n] = th
+        sval[n] = sg
         gated = (th * sg).astype(BF)
-        w_ready(l, (2,))
+        if hh == 0:
+            if l == 0:
+                w_forward(0, (2,))
+            w_ready(l, (2,))
 
         def mixed(j):
             parts = [dot(gated, mw[l, j * ratio + i]) for i in range(ratio)]
             return parts[0] if ratio == 1 else jnp.concatenate(parts, axis=1)
 
         for r in reversed(peers):
-            rsb[l, r] = mixed(peer(r)).astype(BF)
-            rs(l, r, c).start()
-        acc_f[...] = mixed(c) + sig[l, c].astype(F32)
+            rsb[n, r] = mixed(peer(r)).astype(BF)
+            rs(n, r, c).start()
+        acc_f[hh] = mixed(c) + sig[n, c].astype(F32)
+
+    def next_signal(l, hh):
+        n = l * H + hh
+        total = acc_f[hh]
+        for r in peers:
+            rs(n, r, peer(r)).wait_recv()
+            total += rsr[n, peer(r)].astype(F32)
         if l + 1 < layers:
-            w_forward(l + 1)
-        for r in peers:
-            rs(l, r, peer(r)).wait_recv()
-            acc_f[...] += rsr[l, peer(r)].astype(F32)
+            sig[n + H, c] = total.astype(BF)
+            ag_start(n + H, sig.at[n + H, c], sig, n + H)
+        else:
+            out[hh * half:(hh + 1) * half] = total.astype(BF)
+
+    def run(l, first, second):
+        if far(l):
+            for hh in range(H):
+                first(l, hh)
+            for hh in range(H):
+                second(l, hh)
+        else:
+            for hh in range(H):
+                first(l, hh)
+                second(l, hh)
+
+    for l in range(layers):
+        run(l, near_taps, mix_out)
         if l + 1 < layers:
-            sig[l + 1, c] = acc_f[...].astype(BF)
-        else:
-            out[...] = acc_f[...].astype(BF)
-
-    for l in reversed(range(layers)):
-        i = 2 * layers - 1 - l
-        if l < layers - 1:
-            ag_start(i, gr.at[l, c], gr, l)
+            w_forward(l + 1, (0, 1, 2))
+        for hh in range(H):
+            next_signal(l, hh)
+
+    order = list(reversed(peers)) + [0]
+
+    def grads(l, hh):
+        n = l * H + hh
+        i = (2 * layers - 1 - l) * H + hh
         for r in [0] + peers:
             j = peer(r)
             if r:
-                ag_wait(i, gr, l, r)
-            g = gr[l, j]
+                ag_wait(i, gr, n, r)
+            g = gr[n, j]
             for k in range(ratio):
                 z = dot_t(g[:, k * ob:(k + 1) * ob], mw[l, j * ratio + k])
                 if r == 0 and k == 0:
-                    acc_f[...] = z
+                    acc_f[hh] = z
                 else:
-                    acc_f[...] += z
-        gz = acc_f[...]
-        th = tval[l]
-        sg = sval[l]
+                    acc_f[hh] += z
+        gz = acc_f[hh]
+        th = tval[n]
+        sg = sval[n]
         gf = (gz * sg * (1.0 - th * th)).astype(BF)
         gg = (gz * th * sg * (1.0 - sg)).astype(BF)
-        order = list(reversed(peers)) + [0]
+        gf_s[hh] = gf
+        gg_s[hh] = gg
         if far(l):
             @pl.when(m >= span(l))
             def _():
                 for r in order:
                     j = peer(r)
-                    farb[l, j] = (dot_t(gf, block(fw, l, 0, j)) + dot_t(gg, block(gw, l, 0, j))).astype(BF)
-                    fr(l, j).start()
+                    farb[n, j] = (dot_t(gf, block(fw, l, 0, j)) + dot_t(gg, block(gw, l, 0, j))).astype(BF)
+                    fr(l, hh, j).start()
+
+    def sums_out(l, hh):
+        n = l * H + hh
+        i = (2 * layers - 1 - l) * H + hh
+        gf = gf_s[hh]
+        gg = gg_s[hh]
         for r in order:
             j = peer(r)
-            acc_g[...] = dot_t(gf, block(fw, l, 1, j)) + dot_t(gg, block(gw, l, 1, j))
+            acc_g[hh] = dot_t(gf, block(fw, l, 1, j)) + dot_t(gg, block(gw, l, 1, j))
             if far(l):
                 @pl.when(m < tm - span(l))
                 def _():
-                    fr(l, j).wait_recv()
-                    acc_g[...] += farr[l, j].astype(F32)
+                    fr(l, hh, j).wait_recv()
+                    acc_g[hh] += farr[n, j].astype(F32)
             if r:
-                rsb[i, r] = acc_g[...].astype(BF)
+                rsb[i, r] = acc_g[hh].astype(BF)
                 rs(i, r, c).start()
-        acc_f[...] = acc_g[...] + gr[l, c].astype(F32)
+        acc_f[hh] = acc_g[hh] + gr[n, c].astype(F32)
+
+    def next_grad(l, hh):
+        n = l * H + hh
+        i = (2 * layers - 1 - l) * H + hh
+        total = acc_f[hh]
         for r in peers:
             rs(i, r, peer(r)).wait_recv()
-            acc_f[...] += rsr[i, peer(r)].astype(F32)
+            total += rsr[i, peer(r)].astype(F32)
         if l > 0:
-            gr[l - 1, c] = acc_f[...].astype(BF)
+            gr[n - H, c] = total.astype(BF)
+            ag_start(i + H, gr.at[n - H, c], gr, n - H)
         else:
-            gin[...] = acc_f[...].astype(BF)
+            gin[hh * half:(hh + 1) * half] = total.astype(BF)
+
+    for l in reversed(range(layers)):
+        run(l, grads, sums_out)
+        for hh in range(H):
+            next_grad(l, hh)
 
     for l in range(layers):
         for p in range(3):
@@ -301,16 +355,18 @@
         if far(l):
             @pl.when(m < tm - span(l))
             def _():
-                for j in range(chan):
-                    dl(l, j).wait_send()
+                for hh in range(H):
+                    for j in range(chan):
+                        dl(l, hh, j).wait_send()
 
             @pl.when(m >= span(l))
             def _():
-                for j in range(chan):
-                    fr(l, j).wait_send()
-    for i in range(2 * layers):
+                for hh in range(H):
+                    for j in range(chan):
+                        fr(l, hh, j).wait_send()
+    for i in range(2 * layers * H):
         for r in peers:
-            ag(i, rec, sig, 0, r, c).wait_send()
+            ag(i, sig.at[0, c], sig, 0, r, c).wait_send()
             rs(i, r, c).wait_send()
 
 
@@ -322,8 +378,8 @@
     vmem = pl.BlockSpec(memory_space=pltpu.VMEM)
     hbm = pl.BlockSpec(memory_space=pl.ANY)
     weights = pltpu.VMEM((layers, taps, tm, ib, cb), BF)
-    per_layer = pltpu.VMEM((layers, chan, rows, cb), BF)
-    both = pltpu.VMEM((2 * layers, chan, rows, cb), BF)
+    per_layer = pltpu.VMEM((H * layers, chan, rows // H, cb), BF)
+    both = pltpu.VMEM((2 * H * layers, chan, rows // H, cb), BF)
     return pl.pallas_call(
         functools.partial(kernel, layers, tm, chan),
         out_shape=[jax.ShapeDtypeStruct(records.shape, BF)] * 2,
@@ -340,22 +396,24 @@
             per_layer,
             per_layer,
             per_layer,
-            pltpu.VMEM((layers, rows, cb), F32),
-            pltpu.VMEM((layers, rows, cb), F32),
-            pltpu.VMEM((rows, cb), F32),
-            pltpu.VMEM((rows, cb), F32),
+            pltpu.VMEM((H * layers, rows // H, cb), F32),
+            pltpu.VMEM((H * layers, rows // H, cb), F32),
+            pltpu.VMEM((H, rows // H, cb), F32),
+            pltpu.VMEM((H, rows // H, cb), F32),
+            pltpu.VMEM((H, rows // H, cb), BF),
+            pltpu.VMEM((H, rows // H, cb), BF),
             DMA((3 * layers, tm)),
             DMA((3 * layers, tm)),
             DMA((3 * layers, tm)),
             DMA((3 * layers,)),
-            DMA((2 * layers, chan)),
-            DMA((2 * layers, chan)),
-            DMA((layers, chan)),
-            DMA((layers, chan)),
-            DMA((2 * layers, chan)),
-            DMA((2 * layers, chan)),
-            DMA((layers, chan)),
-            DMA((layers, chan)),
+            DMA((2 * H * layers, chan)),
+            DMA((2 * H * layers, chan)),
+            DMA((H * layers, chan)),
+            DMA((H * layers, chan)),
+            DMA((2 * H * layers, chan)),
+            DMA((2 * H * layers, chan)),
+            DMA((H * layers, chan)),
+            DMA((H * layers, chan)),
         ],
         compiler_params=pltpu.CompilerParams(
             collective_id=0, has_side_effects=True, vmem_limit_bytes=56 * 2**20

time: 199 us -> 198 us (level); the launches traced: 195 us -> 198 us
  Pallas kernels: 192 us -> 195 us
    pallas_call x1, Pallas kernels: 192 us -> 195 us  [local(): pl.pallas_call(functools.partial(kernel, layers, tm, chan), out_shape=[ja...]
where the time goes in v2:
time: 198 us
  Pallas kernels  195 us (98%)
  local copies, waits for them, and re-layouts  2.22 us (1%)
    pallas_call x1, Pallas kernels, local(): pl.pallas_call(functools.partial(kernel, layers, tm, chan), out_shape=[ja...  195 us

profile of v2, /device:TPU:0, one launch (start us, length us, event | category | flops | bytes accessed | tf_op | source)
XLA Modules:
  0.0 197.9 jit_solution(14613662517580975785)
XLA Ops:
  0.6 195.0 %shard_map.68 = (bf16[192,256]{1,0:T(8,128)(2,1)}, bf16[192,256]{1,0:T(8,128)(2,1)}) custom-call(bf16[192,256]{1,0:T(8,128)(2,1)} %rec.1, bf16[192,256]{1,0:T(8,128)(2,1)} %cot.1, bf16[4,2,256,256]{3,2,1,0:T(8,128)(2,1)} %f_in.1, bf16[4,2,256,256]{3,2,1,0:T(8,128)(2,1)} %g_in.1, bf16[4,256,256]{2,1,0:T(8,128)(2,1)} %m_in.1), custom_call_target="tpu_custom_call" | custom-call | tf_op jit(solution)/shard_map/pallas_call | solution.py:383
  195.7 0.0 copy-start
  195.7 1.6 copy.9
  197.2 0.0 copy-done
  197.2 0.6 copy.10
Async XLA Ops:
  195.7 1.6 copy-start

commit v3 on v2

--- a/solution.py
+++ b/solution.py
@@ -182,8 +182,6 @@
     for hh in range(H):
         sig[hh, c] = rec[hh * half:(hh + 1) * half]
         gr[(layers - 1) * H + hh, c] = cot[hh * half:(hh + 1) * half]
-    for l in range(1, layers):
-        w_start(l)
     for hh in range(H):
         ag_start(layers * H + hh, cot.at[part(hh)], gr, (layers - 1) * H + hh)
 
@@ -201,6 +199,10 @@
             def _():
                 for r in peers:
                     ag_wait(n, sig, n, r)
+        if hh == H - 1:
+            for later in range(1, layers):
+                if min(later - 1, 1) == l:
+                    w_start(later)
         if hh == 0:
             if l == 0:
                 w_forward(0, (0, 1))
@@ -274,10 +276,10 @@
 
     for l in range(layers):
         run(l, near_taps, mix_out)
+        for hh in range(H):
+            next_signal(l, hh)
         if l + 1 < layers:
             w_forward(l + 1, (0, 1, 2))
-        for hh in range(H):
-            next_signal(l, hh)
 
     order = list(reversed(peers)) + [0]
 

time: 198 us -> 162 us (0.82)
  Pallas kernels: 195 us -> 159 us
    pallas_call x1, Pallas kernels: 195 us -> 159 us  [local(): pl.pallas_call(functools.partial(kernel, layers, tm, chan), out_shape=[ja...]
where the time goes in v3:
time: 162 us
  Pallas kernels  159 us (98%)
  local copies, waits for them, and re-layouts  2.22 us (1%)
    pallas_call x1, Pallas kernels, local(): pl.pallas_call(functools.partial(kernel, layers, tm, chan), out_shape=[ja...  159 us

profile of v3, /device:TPU:0, one launch (start us, length us, event | category | flops | bytes accessed | tf_op | source)
XLA Modules:
  0.0 162.2 jit_solution(9198718621169364407)
XLA Ops:
  0.6 159.3 %shard_map.68 = (bf16[192,256]{1,0:T(8,128)(2,1)}, bf16[192,256]{1,0:T(8,128)(2,1)}) custom-call(bf16[192,256]{1,0:T(8,128)(2,1)} %rec.1, bf16[192,256]{1,0:T(8,128)(2,1)} %cot.1, bf16[4,2,256,256]{3,2,1,0:T(8,128)(2,1)} %f_in.1, bf16[4,2,256,256]{3,2,1,0:T(8,128)(2,1)} %g_in.1, bf16[4,256,256]{2,1,0:T(8,128)(2,1)} %m_in.1), custom_call_target="tpu_custom_call" | custom-call | tf_op jit(solution)/shard_map/pallas_call | solution.py:385
  159.9 0.0 copy-start
  159.9 1.6 copy.9
  161.5 0.0 copy-done
  161.5 0.6 copy.10
Async XLA Ops:
  159.9 1.6 copy-start

commit v4 on v3

--- a/solution.py
+++ b/solution.py
@@ -37,7 +37,7 @@
     out, gin,
     fw, gw, mw, sig, dly, rsb, rsr, gr, farb, farr, tval, sval, acc_f, acc_g, gf_s, gg_s,
     w_send, w_recv, w_fwd, w_own,
-    ag_send, ag_recv, d_send, d_recv, rs_send, rs_recv, f_send, f_recv,
+    ag_send, ag_fwd, ag_recv, d_send, d_recv, rs_send, rs_recv, f_send, f_recv,
 ):
     m = lax.axis_index("tm")
     c = lax.axis_index("chan")
@@ -48,6 +48,8 @@
     partner = m + 1 - 2 * lax.rem(m, 2)
     peers = near_first(chan)
     others = list(range(1, tm // 2))
+    seconds = list(range(1, chan // 2))
+    pair = c + 1 - 2 * lax.rem(c, 2)
 
     def peer(r):
         return lax.rem(c + r, chan)
@@ -114,22 +116,39 @@
                 s = mate(q, partner)
                 w_copy(l, p, s, partner, w_fwd.at[l * 3 + p, 0], False).wait_recv()
 
-    def ag(i, src, buf, l, r, owner):
+    def ag(i, src, buf, l, to, owner, send):
         return pltpu.make_async_remote_copy(
             src_ref=src,
             dst_ref=buf.at[l, owner],
-            send_sem=ag_send.at[i, r],
+            send_sem=send,
             recv_sem=ag_recv.at[i, owner],
-            device_id={"chan": peer(r)},
+            device_id={"chan": to},
             device_id_type=MESH,
         )
 
+    def ag_out(i, src, buf, l, q):
+        return ag(i, src, buf, l, peer(2 * q) if q else pair, c, ag_send.at[i, q])
+
+    def ag_on(i, buf, l, q):
+        return ag(i, buf.at[l, peer(2 * q)], buf, l, pair, peer(2 * q), ag_fwd.at[i, q])
+
     def ag_start(i, src, buf, l):
-        for r in reversed(peers):
-            ag(i, src, buf, l, r, c).start()
-
-    def ag_wait(i, buf, l, r):
-        ag(i, buf.at[l, c], buf, l, r, peer(r)).wait_recv()
+        for q in seconds + [0]:
+            ag_out(i, src, buf, l, q).start()
+
+    def ag_relay(i, buf, l):
+        for q in seconds:
+            ag_on(i, buf, l, q).wait_recv()
+            ag_on(i, buf, l, q).start()
+
+    def ag_wait(i, buf, l, j):
+        ag(i, buf.at[l, c], buf, l, pair, j, ag_send.at[i, 0]).wait_recv()
+
+    def here():
+        return [c] + [peer(2 * q) for q in seconds]
+
+    def coming():
+        return [pair] + [lax.rem(pair + 2 * q, chan) for q in seconds]
 
     def rs(i, r, owner):
         return pltpu.make_async_remote_copy(
@@ -190,15 +209,16 @@
         if far(l):
             @pl.when(m < tm - span(l))
             def _():
-                dl(l, hh, c).start()
-                for r in peers:
-                    ag_wait(n, sig, n, r)
-                    dl(l, hh, peer(r)).start()
+                for j in here():
+                    dl(l, hh, j).start()
+                for j in coming():
+                    ag_wait(n, sig, n, j)
+                    dl(l, hh, j).start()
 
             @pl.when(m >= tm - span(l))
             def _():
-                for r in peers:
-                    ag_wait(n, sig, n, r)
+                for j in coming():
+                    ag_wait(n, sig, n, j)
         if hh == H - 1:
             for later in range(1, layers):
                 if min(later - 1, 1) == l:
@@ -207,10 +227,9 @@
             if l == 0:
                 w_forward(0, (0, 1))
             w_ready(l, (0, 1))
-        for r in [0] + peers:
-            j = peer(r)
-            if r and not far(l):
-                ag_wait(n, sig, n, r)
+        for r, j in enumerate(here() + coming()):
+            if r >= chan // 2 and not far(l):
+                ag_wait(n, sig, n, j)
             x = sig[n, j]
             a = dot(x, block(fw, l, 1, j))
             b = dot(x, block(gw, l, 1, j))
@@ -226,8 +245,7 @@
         if far(l):
             @pl.when(m >= span(l))
             def _():
-                for r in [0] + peers:
-                    j = peer(r)
+                for j in here() + coming():
                     dl(l, hh, j).wait_recv()
                     x = dly[n, j]
                     acc_f[hh] += dot(x, block(fw, l, 0, j))
@@ -275,6 +293,11 @@
                 second(l, hh)
 
     for l in range(layers):
+        for hh in range(H):
+            ag_relay(l * H + hh, sig, l * H + hh)
+        if l == 1 or layers == 1:
+            for hh in range(H):
+                ag_relay(layers * H + hh, gr, (layers - 1) * H + hh)
         run(l, near_taps, mix_out)
         for hh in range(H):
             next_signal(l, hh)
@@ -286,10 +309,9 @@
     def grads(l, hh):
         n = l * H + hh
         i = (2 * layers - 1 - l) * H + hh
-        for r in [0] + peers:
-            j = peer(r)
-            if r:
-                ag_wait(i, gr, n, r)
+        for r, j in enumerate(here() + coming()):
+            if r >= chan // 2:
+                ag_wait(i, gr, n, j)
             g = gr[n, j]
             for k in range(ratio):
                 z = dot_t(g[:, k * ob:(k + 1) * ob], mw[l, j * ratio + k])
@@ -344,6 +366,9 @@
             gin[hh * half:(hh + 1) * half] = total.astype(BF)
 
     for l in reversed(range(layers)):
+        if l < layers - 1:
+            for hh in range(H):
+                ag_relay((2 * layers - 1 - l) * H + hh, gr, l * H + hh)
         run(l, grads, sums_out)
         for hh in range(H):
             next_grad(l, hh)
@@ -367,8 +392,11 @@
                     for j in range(chan):
                         fr(l, hh, j).wait_send()
     for i in range(2 * layers * H):
+        for q in seconds:
+            ag_on(i, sig, 0, q).wait_send()
+        for q in [0] + seconds:
+            ag_out(i, sig.at[0, c], sig, 0, q).wait_send()
         for r in peers:
-            ag(i, sig.at[0, c], sig, 0, r, c).wait_send()
             rs(i, r, c).wait_send()
 
 
@@ -410,6 +438,7 @@
             DMA((3 * layers,)),
             DMA((2 * H * layers, chan)),
             DMA((2 * H * layers, chan)),
+            DMA((2 * H * layers, chan)),
             DMA((H * layers, chan)),
             DMA((H * layers, chan)),
             DMA((2 * H * layers, chan)),

time: 162 us -> 155 us (0.957); the launches traced: 162 us -> 153 us
  Pallas kernels: 159 us -> 150 us
    pallas_call x1, Pallas kernels: 159 us -> 150 us  [local(): pl.pallas_call(functools.partial(kernel, layers, tm, chan), out_shape=[ja...]
where the time goes in v4:
time: 155 us; the launch traced here: 153 us
  Pallas kernels  150 us (97%)
  local copies, waits for them, and re-layouts  2.22 us (1%)
    pallas_call x1, Pallas kernels, local(): pl.pallas_call(functools.partial(kernel, layers, tm, chan), out_shape=[ja...  150 us

profile of v4, /device:TPU:0, one launch (start us, length us, event | category | flops | bytes accessed | tf_op | source)
XLA Modules:
  0.0 153.4 jit_solution(13142884738954318197)
XLA Ops:
  0.6 150.5 %shard_map.68 = (bf16[192,256]{1,0:T(8,128)(2,1)}, bf16[192,256]{1,0:T(8,128)(2,1)}) custom-call(bf16[192,256]{1,0:T(8,128)(2,1)} %rec.1, bf16[192,256]{1,0:T(8,128)(2,1)} %cot.1, bf16[4,2,256,256]{3,2,1,0:T(8,128)(2,1)} %f_in.1, bf16[4,2,256,256]{3,2,1,0:T(8,128)(2,1)} %g_in.1, bf16[4,256,256]{2,1,0:T(8,128)(2,1)} %m_in.1), custom_call_target="tpu_custom_call" | custom-call | tf_op jit(solution)/shard_map/pallas_call | solution.py:413
  151.1 0.0 copy-start
  151.1 1.6 %copy.9 = bf16[192,256]{1,0:T(8,128)(2,1)} copy(bf16[192,256]{1,0:T(8,128)(2,1)} %get-tuple-element.4) | data formatting | bytes 196608
  152.7 0.0 copy-done
  152.7 0.6 copy.10
Async XLA Ops:
  151.1 1.6 %copy-start = (bf16[192,256]{1,0:T(8,128)(2,1)S(1)}, bf16[192,256]{1,0:T(8,128)(2,1)}, u32[]{:S(2)}) copy-start(bf16[192,256]{1,0:T(8,128)(2,1)} %get-tuple-element.5) | copy-start | bytes 294916
